TPU v7x, 256 devices: a whole 4x4x8 slice. The times are simulated.
256 devices in a mesh: rep: 4 (over y), fsdp: 64 (over x, z, core).
Axes of the slice: x: 4, y: 4, z: 8, core: 2. Of those that a mesh axis runs over, the one named last changes fastest.
Arguments:
- activations: bfloat16 [65536, 512], P(('rep', 'fsdp')), may hold values from -6 to 6
- output_grads: bfloat16 [65536, 8192], P(('rep', 'fsdp'))
- master: float32 [8192, 512], P('fsdp'), may hold values from -6 to 6
- first_moment: float32 [8192, 512], P('fsdp'), may hold values from -4 to 4
- second_moment: float32 [8192, 512], P('fsdp'), may hold values from 0.2 to 2
Outputs:
- new_master: float32 [8192, 512], P('fsdp')
- new_first: float32 [8192, 512], P('fsdp')
- new_second: float32 [8192, 512], P('fsdp')
- params: bfloat16 [8192, 512], replicated
All inputs are finite; a program needn't handle non-finite values.
Results may differ from a plain program's by a relative error of at most 0.0004.
Values may be sent and summed in bfloat16 or wider, within the bound.
No kernel may reach another device: no remote copies, remote signals or barrier semaphores. Data moves between devices by JAX's collectives and lax.ppermute only.
A program may use at most 128 MiB of HBM per device.

v0:
```python
import jax
import jax.numpy as jnp
from jax import lax
from jax.sharding import Mesh, PartitionSpec as P

dot_epsilon = 1e-06
beta_one = 0.9
beta_two = 0.95
adam_epsilon = 1e-08
learn_rate = 0.02
decay_rate = 0.1
contract_first = (((0,), (0,)), ((), ()))
GROUP = ("x", "z", "core")


def shifted(value, axis, step):
    size = lax.axis_size(axis)
    return lax.ppermute(value, axis, [(i, (i + step) % size) for i in range(size)])


def add_top(whole, part):
    rows = part.shape[0]
    return jnp.concatenate([whole[:rows] + part, whole[rows:]], axis=0)


def add_bottom(whole, part):
    rows = whole.shape[0] - part.shape[0]
    return jnp.concatenate([whole[:rows], whole[rows:] + part], axis=0)


def ring_reduce(chunk, axis):
    size = lax.axis_size(axis)
    half = size // 2
    far = chunk(half)
    rows = far.shape[0] // 2
    up = shifted(far[:rows], axis, 1)
    down = shifted(far[rows:], axis, -1)
    for reach in range(half - 1, 0, -1):
        if reach == half - 1:
            send_up, send_down = (add_top(chunk(reach), up), add_bottom(chunk(-reach), down))
        else:
            send_up, send_down = (chunk(reach) + up, chunk(-reach) + down)
        up = shifted(send_up, axis, 1)
        down = shifted(send_down, axis, -1)
    return chunk(0) + up + down


def by_place(whole, axis):
    size = lax.axis_size(axis)
    place = lax.axis_index(axis)

    def chunk(step):
        return lax.dynamic_index_in_dim(whole, (place + step + size) % size, 0, keepdims=False)

    return chunk


def group_members(own):
    place = lax.axis_index("rep")
    below, above, across = (shifted(own, "rep", 1), shifted(own, "rep", -1), shifted(own, "rep", 2))
    members = []
    for member in range(4):
        value = jnp.where(
            place == member,
            own,
            jnp.where(
                place == (member + 1) % 4,
                below,
                jnp.where(place == (member + 3) % 4, above, across),
            ),
        )
        members.append(value)
    return members


def pair_coefs(cross, left_sq, right_sq):
    return (
        1.0 - cross / (2.0 * (left_sq + dot_epsilon)),
        1.0 - cross / (2.0 * (right_sq + dot_epsilon)),
    )


def local(activations, output_grads, master, first_moment, second_moment):
    core = lax.axis_index("core")
    x_place = lax.axis_index("x")
    tokens, features = output_grads.shape
    width = activations.shape[1]
    rows = master.shape[0]
    half = width // 2
    with jax.named_scope("core_swap"):
        by_core = output_grads.reshape(tokens, features // (2 * rows), 2, rows)
        kept = jnp.where(core == 0, by_core[:, :, 0], by_core[:, :, 1]).reshape(
            tokens, features // 2
        )
        given = jnp.where(core == 0, by_core[:, :, 1], by_core[:, :, 0]).reshape(
            tokens, features // 2
        )
        grads = jnp.concatenate([kept, shifted(given, "core", 1)], axis=0)
        acts = jnp.concatenate([activations, shifted(activations, "core", 1)], axis=0)

    def product(grad_columns, act_columns):
        return lax.dot_general(
            grad_columns, act_columns, contract_first, preferred_element_type=jnp.float32
        )

    with jax.named_scope("reduce_b"):
        sums_b = product(grads, acts[:, half:]).reshape(4, 8, rows, half)
        sums_b = jnp.swapaxes(sums_b, 0, 1).reshape(8 * 4 * rows, half)
        sums_b = lax.psum_scatter(sums_b, "z", scatter_dimension=0, tiled=True)
    with jax.named_scope("reduce_a"):
        strip = features // 8

        def chunk_a(step):
            place = (x_place + step + 4) % 4
            return product(lax.dynamic_slice_in_dim(grads, place * strip, strip, 1), acts[:, :half])

        sums_a = ring_reduce(chunk_a, "x").reshape(8, rows, half)
        grad_a = ring_reduce(by_place(sums_a, "z"), "z")
    with jax.named_scope("reduce_b2"):
        grad_b = ring_reduce(by_place(sums_b.reshape(4, rows, half), "x"), "x")
    with jax.named_scope("members"):
        members_a = group_members(grad_a)
        members_b = group_members(grad_b)
        members = [jnp.concatenate(pair, axis=1) for pair in zip(members_a, members_b)]
    with jax.named_scope("gram"):
        pairs = [(i, j) for i in range(4) for j in range(i, 4)]
        sums = [jnp.sum(members[i] * members[j]) for i, j in pairs]
        row = jnp.concatenate([jnp.stack(sums), jnp.zeros((128 - len(sums),), jnp.float32)])
        everyone = lax.all_to_all(jnp.broadcast_to(row, (64, 1, 128)), GROUP, 0, 0)
        totals = jnp.sum(everyone, axis=(0, 1))
        gram = {pair: totals[index] for index, pair in enumerate(pairs)}
    with jax.named_scope("combine"):
        c0, c1 = pair_coefs(gram[0, 1], gram[0, 0], gram[1, 1])
        c2, c3 = pair_coefs(gram[2, 3], gram[2, 2], gram[3, 3])
        low_sq = c0 * c0 * gram[0, 0] + 2.0 * c0 * c1 * gram[0, 1] + c1 * c1 * gram[1, 1]
        high_sq = c2 * c2 * gram[2, 2] + 2.0 * c2 * c3 * gram[2, 3] + c3 * c3 * gram[3, 3]
        cross = c0 * (c2 * gram[0, 2] + c3 * gram[0, 3]) + c1 * (c2 * gram[1, 2] + c3 * gram[1, 3])
        low, high = pair_coefs(cross, jnp.maximum(low_sq, 0.0), jnp.maximum(high_sq, 0.0))
        combined = low * (c0 * members[0] + c1 * members[1]) + high * (
            c2 * members[2] + c3 * members[3]
        )
    with jax.named_scope("adamw"):
        correct_one = 1.0 - (beta_one**50) ** 2
        correct_two = 1.0 - (beta_two**50) ** 2
        new_first = beta_one * first_moment + (1.0 - beta_one) * combined
        new_second = beta_two * second_moment + (1.0 - beta_two) * combined * combined
        update = (
            new_first / correct_one / (jnp.sqrt(new_second / correct_two) + adam_epsilon)
            + decay_rate * master
        )
        new_master = master - learn_rate * update
    with jax.named_scope("params"):
        params = lax.all_gather(new_master.astype(jnp.bfloat16), GROUP, axis=0, tiled=True)
    return (new_master, new_first, new_second, params)


def solution(mesh):
    fine = Mesh(mesh.devices.reshape(4, 4, 8, 2), ("rep",) + GROUP)
    everyone = P(("rep",) + GROUP, None)
    block = P(GROUP, None)
    return jax.shard_map(
        local,
        mesh=fine,
        in_specs=(everyone, everyone, block, block, block),
        out_specs=(block, block, block, P()),
        check_vma=False,
    )
```

profile of v0, /device:TPU:1, one launch (start us, length us, event | category | flops | bytes accessed | tf_op | source)
XLA Modules:
  0.0 256.1 jit_solution(2416143929010002792)
XLA Ops:
  7.2 6.4 %copy.14 = bf16[256,8192]{0,1:T(8,128)(2,1)} copy(bf16[256,8192]{1,0:T(8,128)(2,1)} %param.6) | data formatting | bytes 8388608 | tf_op args[1]
  13.6 2.5 broadcast_select_fusion.1
  16.1 3.3 %collective-permute-start = (bf16[256,4096]{0,1:T(8,128)(2,1)S(1)}, bf16[256,4096]{0,1:T(8,128)(2,1)S(1)}, u32[]{:S(2)}, u32[]{:S(2)}) collective-permute-start(bf16[256,4096]{0,1:T(8,128)(2,1)S(1)} %bitcast.92), channel_id=1, source_target_pairs={{0,1},{1,0},{2,3},{3,2},{4,5},{5,4},{6,7},{7,6},{8,9},{9,8},{10,11... | collective-permute-start | bytes 6291464 | tf_op jit(solution)/shard_map/core_swap/ppermute | solution.py:18
  19.6 4.0 %collective-permute-done.1 = bf16[256,512]{1,0:T(8,128)(2,1)S(1)} collective-permute-done((bf16[256,512]{1,0:T(8,128)(2,1)S(1)}, bf16[256,512]{1,0:T(8,128)(2,1)S(1)}, u32[]{:S(2)}, u32[]{:S(2)}) %collective-permute-start.1) | collective-permute-done | bytes 262176 | tf_op jit(solution)/shard_map/core_swap/ppermute | solution.py:18
  23.7 1.3 fusion
  25.0 2.3 copy.15
  27.4 1.5 fusion.8
  31.4 1.5 fusion.5
  33.3 10.0 %collective-permute-done.4 = f32[512,256]{1,0:T(8,128)S(1)} collective-permute-done((f32[512,256]{1,0:T(8,128)}, f32[512,256]{1,0:T(8,128)S(1)}, u32[]{:S(2)}, u32[]{:S(2)}) %collective-permute-start.4) | collective-permute-done | bytes 524320 | tf_op jit(solution)/shard_map/reduce_a/ppermute | solution.py:18
  43.6 1.9 collective-permute-start.5
  46.6 20.6 %collective-permute-done.5 = f32[1024,256]{1,0:T(8,128)} collective-permute-done((f32[1024,256]{1,0:T(8,128)S(1)}, f32[1024,256]{1,0:T(8,128)}, u32[]{:S(2)}, u32[]{:S(2)}) %collective-permute-start.5) | collective-permute-done | bytes 1048608 | tf_op jit(solution)/shard_map/reduce_a/ppermute | solution.py:18
  67.3 4.0 %collective-permute-done.3 = f32[1024,256]{1,0:T(8,128)} collective-permute-done((f32[1024,256]{1,0:T(8,128)}, f32[1024,256]{1,0:T(8,128)}, u32[]{:S(2)}, u32[]{:S(2)}) %collective-permute-start.3) | collective-permute-done | bytes 1048608 | tf_op jit(solution)/shard_map/reduce_a/ppermute | solution.py:18
  71.3 2.2 fusion.1
  73.6 1.7 collective-permute-start.6
  75.3 4.3 %collective-permute-start.10 = (f32[64,256]{1,0:T(8,128)S(1)}, f32[64,256]{1,0:T(8,128)S(1)}, u32[]{:S(2)}, u32[]{:S(2)}) collective-permute-start(f32[64,256]{1,0:T(8,128)S(1)} %get-tuple-element.26), channel_id=1, source_target_pairs={{0,14},{2,0},{4,2},{6,4},{8,6},{10,8},{12,10},{14,12},{1,15},{3,1}... | collective-permute-start | bytes 196616 | tf_op jit(solution)/shard_map/reduce_a/ppermute | solution.py:18
  79.6 3.5 %collective-permute-done.6 = f32[64,256]{1,0:T(8,128)S(1)} collective-permute-done((f32[64,256]{1,0:T(8,128)S(1)}, f32[64,256]{1,0:T(8,128)S(1)}, u32[]{:S(2)}, u32[]{:S(2)}) %collective-permute-start.6) | collective-permute-done | bytes 65568 | tf_op jit(solution)/shard_map/reduce_a/ppermute | solution.py:18
  83.3 2.7 %collective-permute-start.11 = (f32[128,256]{1,0:T(8,128)S(1)}, f32[128,256]{1,0:T(8,128)S(1)}, u32[]{:S(2)}, u32[]{:S(2)}) collective-permute-start(f32[128,256]{1,0:T(8,128)S(1)} %pad_maximum_fusion.9), channel_id=1, source_target_pairs={{0,14},{2,0},{4,2},{6,4},{8,6},{10,8},{12,10},{14,12},{1,15},{3,1}... | collective-permute-start | bytes 393224 | tf_op jit(solution)/shard_map/reduce_a/ppermute | solution.py:18
  86.0 2.3 collective-permute-done.7
  88.6 5.0 %collective-permute-done.8 = f32[128,256]{1,0:T(8,128)S(1)} collective-permute-done((f32[128,256]{1,0:T(8,128)S(1)}, f32[128,256]{1,0:T(8,128)S(1)}, u32[]{:S(2)}, u32[]{:S(2)}) %collective-permute-start.8) | collective-permute-done | bytes 131104 | tf_op jit(solution)/shard_map/reduce_a/ppermute | solution.py:18
  93.8 1.4 collective-permute-start.9
  96.2 2.7 %collective-permute-start.19 = (f32[64,256]{1,0:T(8,128)S(1)}, f32[64,256]{1,0:T(8,128)S(1)}, u32[]{:S(2)}, u32[]{:S(2)}) collective-permute-start(f32[64,256]{1,0:T(8,128)S(1)} %get-tuple-element.50), channel_id=1, source_target_pairs={{0,48},{16,0},{32,16},{48,32},{1,49},{17,1},{33,17},{49,33},{2,50}... | collective-permute-start | bytes 196616 | tf_op jit(solution)/shard_map/reduce_b2/ppermute | solution.py:18
  98.9 1.5 collective-permute-start.13
  101.4 3.0 %collective-permute-start.20 = (f32[128,256]{1,0:T(8,128)S(1)}, f32[128,256]{1,0:T(8,128)S(1)}, u32[]{:S(2)}, u32[]{:S(2)}) collective-permute-start(f32[128,256]{1,0:T(8,128)S(1)} %pad_maximum_fusion.11), channel_id=1, source_target_pairs={{0,48},{16,0},{32,16},{48,32},{1,49},{17,1},{33,17},{49,33},{2,50}... | collective-permute-start | bytes 393224 | tf_op jit(solution)/shard_map/reduce_b2/ppermute | solution.py:18
  104.7 3.0 %collective-permute-start.16 = (f32[128,256]{1,0:T(8,128)S(1)}, f32[128,256]{1,0:T(8,128)S(1)}, u32[]{:S(2)}, u32[]{:S(2)}) collective-permute-start(f32[128,256]{1,0:T(8,128)S(1)} %fusion.20), channel_id=1, source_target_pairs={{0,128},{64,192},{128,0},{192,64},{1,129},{65,193},{129,1},{193,65... | collective-permute-start | bytes 393224 | tf_op jit(solution)/shard_map/members/ppermute | solution.py:18
  110.5 3.0 %collective-permute-start.23 = (f32[128,256]{1,0:T(8,128)S(1)}, f32[128,256]{1,0:T(8,128)S(1)}, u32[]{:S(2)}, u32[]{:S(2)}) collective-permute-start(f32[128,256]{1,0:T(8,128)S(1)} %fusion.19), channel_id=1, source_target_pairs={{0,128},{64,192},{128,0},{192,64},{1,129},{65,193},{129,1},{193,65... | collective-permute-start | bytes 393224 | tf_op jit(solution)/shard_map/members/ppermute | solution.py:18
  115.1 1.6 collective-permute-done.23
  116.7 2.5 collective-permute-done.22
  120.3 6.4 %concatenate.51 = f32[128]{0:T(128)S(1)} concatenate(f32[1]{0:T(128)} %bitcast.26, f32[1]{0:T(128)} %bitcast.27, f32[1]{0:T(128)} %bitcast.28, f32[1]{0:T(128)} %bitcast.29, f32[1]{0:T(128)} %bitcast.30, f32[1]{0:T(128)} %bitcast.31, f32[1]{0:T(128)} %bitcast.32, f32[1]{0:T(128)} %bitcast.33, f32[1]{0:T(128)} %bitcast.34, f32[1]{0:T(128)} %bitcast.35, f32[118]{0:T(128)S(1)} %broadcast_in_dim.6), dimensions={0} | concatenate | bytes 1024 | tf_op jit(solution)/shard_map/gram/concatenate | solution.py:128
  126.8 25.9 %all_to_all.5 = f32[64,1,128]{2,1,0:T(1,128)S(1)} all-to-all(f32[64,1,128]{2,1,0:T(1,128)S(1)} %broadcast_in_dim.7), channel_id=1, replica_groups=mesh['rep'=4,'x'=4,'z'=8,'core'=2] {'x','z','core'}, dimensions={0} | all-to-all | bytes 65536 | tf_op jit(solution)/shard_map/gram/all_to_all | solution.py:129
  164.9 1.1 fusion.34
  166.0 75.9 %all-gather.2.cloned.1.call-done = bf16[8192,512]{1,0:T(8,128)(2,1)} async-done(((bf16[128,512]{1,0:T(8,128)(2,1)}), bf16[8192,512]{1,0:T(8,128)(2,1)}) %all-gather.2.cloned.1.call-update) | async-done | bytes 8388624 | tf_op jit(solution)/shard_map/params/all_gather | solution.py:153
  241.9 7.3 %copy.19 = bf16[8192,512]{1,0:T(8,128)(2,1)} copy(bf16[8192,512]{1,0:T(8,128)(2,1)} %all-gather.2.cloned.1.call-done) | data formatting | bytes 16777216
  (75 shorter events, 13.7 us)
Async XLA Ops:
  7.2 88.0 %reduce-scatter.2.cloned.1.call-start = ((), (), s32[]{:S(2)}) async-start(), calls=%async_computation.2 | async-start | bytes 4718592 | tf_op jit(solution)/shard_map/reduce_b/reduce_scatter | solution.py:109
  13.6 5.9 %copy-start.6 = (bf16[256,512]{1,0:T(8,128)(2,1)S(1)}, bf16[256,512]{1,0:T(8,128)(2,1)}, u32[]{:S(2)}) copy-start(bf16[256,512]{1,0:T(8,128)(2,1)} %param.5) | copy-start | bytes 786436
  16.1 7.5 %collective-permute-start = (bf16[256,4096]{0,1:T(8,128)(2,1)S(1)}, bf16[256,4096]{0,1:T(8,128)(2,1)S(1)}, u32[]{:S(2)}, u32[]{:S(2)}) collective-permute-start(bf16[256,4096]{0,1:T(8,128)(2,1)S(1)} %bitcast.92), channel_id=1, source_target_pairs={{0,1},{1,0},{2,3},{3,2},{4,5},{5,4},{6,7},{7,6},{8,9},{9,8},{10,11... | collective-permute-start | bytes 6291464 | tf_op jit(solution)/shard_map/core_swap/ppermute | solution.py:18
  19.5 4.2 %collective-permute-start.1 = (bf16[256,512]{1,0:T(8,128)(2,1)S(1)}, bf16[256,512]{1,0:T(8,128)(2,1)S(1)}, u32[]{:S(2)}, u32[]{:S(2)}) collective-permute-start(bf16[256,512]{1,0:T(8,128)(2,1)S(1)} %copy-done.6), channel_id=1, source_target_pairs={{0,1},{1,0},{2,3},{3,2},{4,5},{5,4},{6,7},{7,6},{8,9},{9,8},{10,11... | collective-permute-start | bytes 786440 | tf_op jit(solution)/shard_map/core_swap/ppermute | solution.py:18
  23.6 9.2 %copy-start.2 = (bf16[512,512]{1,0:T(8,128)(2,1)}, bf16[512,512]{1,0:T(8,128)(2,1)S(1)}, u32[]{:S(2)}) copy-start(bf16[512,512]{1,0:T(8,128)(2,1)S(1)} %constant_dynamic-update-slice_fusion) | copy-start | bytes 1572868
  27.3 214.6 %all-gather.2.cloned.1.call-start = ((), (), s32[]{:S(2)}) async-start(), calls=%async_computation.3 | async-start | bytes 8519680 | tf_op jit(solution)/shard_map/params/all_gather | solution.py:153
  29.9 13.4 %collective-permute-start.4 = (f32[512,256]{1,0:T(8,128)}, f32[512,256]{1,0:T(8,128)S(1)}, u32[]{:S(2)}, u32[]{:S(2)}) collective-permute-start(f32[512,256]{1,0:T(8,128)} %get-tuple-element.31), channel_id=1, source_target_pairs={{0,48},{16,0},{32,16},{48,32},{1,49},{17,1},{33,17},{49,33},{2,50}... | collective-permute-start | bytes 1572872 | tf_op jit(solution)/shard_map/reduce_a/ppermute | solution.py:18
  30.7 2.2 copy-start.1
  30.7 14.8 %collective-permute-start.2 = (f32[512,256]{1,0:T(8,128)}, f32[512,256]{1,0:T(8,128)S(1)}, u32[]{:S(2)}, u32[]{:S(2)}) collective-permute-start(f32[512,256]{1,0:T(8,128)} %get-tuple-element.30), channel_id=1, source_target_pairs={{0,16},{16,32},{32,48},{48,0},{1,17},{17,33},{33,49},{49,1},{2,18}... | collective-permute-start | bytes 1572872 | tf_op jit(solution)/shard_map/reduce_a/ppermute | solution.py:18
  43.6 23.7 %collective-permute-start.5 = (f32[1024,256]{1,0:T(8,128)S(1)}, f32[1024,256]{1,0:T(8,128)}, u32[]{:S(2)}, u32[]{:S(2)}) collective-permute-start(f32[1024,256]{1,0:T(8,128)S(1)} %pad_maximum_fusion.3), channel_id=1, source_target_pairs={{0,48},{16,0},{32,16},{48,32},{1,49},{17,1},{33,17},{49,33},{2,50}... | collective-permute-start | bytes 3145736 | tf_op jit(solution)/shard_map/reduce_a/ppermute | solution.py:18
  46.6 24.7 %collective-permute-start.3 = (f32[1024,256]{1,0:T(8,128)}, f32[1024,256]{1,0:T(8,128)}, u32[]{:S(2)}, u32[]{:S(2)}) collective-permute-start(f32[1024,256]{1,0:T(8,128)} %pad_maximum_fusion.2), channel_id=1, source_target_pairs={{0,16},{16,32},{32,48},{48,0},{1,17},{17,33},{33,49},{49,1},{2,18}... | collective-permute-start | bytes 3145736 | tf_op jit(solution)/shard_map/reduce_a/ppermute | solution.py:18
  73.6 9.5 %collective-permute-start.6 = (f32[64,256]{1,0:T(8,128)S(1)}, f32[64,256]{1,0:T(8,128)S(1)}, u32[]{:S(2)}, u32[]{:S(2)}) collective-permute-start(f32[64,256]{1,0:T(8,128)S(1)} %get-tuple-element.24), channel_id=1, source_target_pairs={{0,2},{2,4},{4,6},{6,8},{8,10},{10,12},{12,14},{14,0},{1,3},{3,5},... | collective-permute-start | bytes 196616 | tf_op jit(solution)/shard_map/reduce_a/ppermute | solution.py:18
  75.3 7.8 %collective-permute-start.10 = (f32[64,256]{1,0:T(8,128)S(1)}, f32[64,256]{1,0:T(8,128)S(1)}, u32[]{:S(2)}, u32[]{:S(2)}) collective-permute-start(f32[64,256]{1,0:T(8,128)S(1)} %get-tuple-element.26), channel_id=1, source_target_pairs={{0,14},{2,0},{4,2},{6,4},{8,6},{10,8},{12,10},{14,12},{1,15},{3,1}... | collective-permute-start | bytes 196616 | tf_op jit(solution)/shard_map/reduce_a/ppermute | solution.py:18
  83.2 5.1 %collective-permute-start.7 = (f32[128,256]{1,0:T(8,128)S(1)}, f32[128,256]{1,0:T(8,128)S(1)}, u32[]{:S(2)}, u32[]{:S(2)}) collective-permute-start(f32[128,256]{1,0:T(8,128)S(1)} %pad_maximum_fusion.8), channel_id=1, source_target_pairs={{0,2},{2,4},{4,6},{6,8},{8,10},{10,12},{12,14},{14,0},{1,3},{3,5},... | collective-permute-start | bytes 393224 | tf_op jit(solution)/shard_map/reduce_a/ppermute | solution.py:18
  83.3 5.3 %collective-permute-start.11 = (f32[128,256]{1,0:T(8,128)S(1)}, f32[128,256]{1,0:T(8,128)S(1)}, u32[]{:S(2)}, u32[]{:S(2)}) collective-permute-start(f32[128,256]{1,0:T(8,128)S(1)} %pad_maximum_fusion.9), channel_id=1, source_target_pairs={{0,14},{2,0},{4,2},{6,4},{8,6},{10,8},{12,10},{14,12},{1,15},{3,1}... | collective-permute-start | bytes 393224 | tf_op jit(solution)/shard_map/reduce_a/ppermute | solution.py:18
  88.3 5.3 %collective-permute-start.8 = (f32[128,256]{1,0:T(8,128)S(1)}, f32[128,256]{1,0:T(8,128)S(1)}, u32[]{:S(2)}, u32[]{:S(2)}) collective-permute-start(f32[128,256]{1,0:T(8,128)S(1)} %bitcast_add_fusion.3), channel_id=1, source_target_pairs={{0,2},{2,4},{4,6},{6,8},{8,10},{10,12},{12,14},{14,0},{1,3},{3,5},... | collective-permute-start | bytes 393224 | tf_op jit(solution)/shard_map/reduce_a/ppermute | solution.py:18
  93.6 5.3 %collective-permute-start.12 = (f32[128,256]{1,0:T(8,128)S(1)}, f32[128,256]{1,0:T(8,128)S(1)}, u32[]{:S(2)}, u32[]{:S(2)}) collective-permute-start(f32[128,256]{1,0:T(8,128)S(1)} %get-tuple-element.21), channel_id=1, source_target_pairs={{0,14},{2,0},{4,2},{6,4},{8,6},{10,8},{12,10},{14,12},{1,15},{3,1}... | collective-permute-start | bytes 393224 | tf_op jit(solution)/shard_map/reduce_a/ppermute | solution.py:18
  93.8 10.8 %collective-permute-start.9 = (f32[128,256]{1,0:T(8,128)S(1)}, f32[128,256]{1,0:T(8,128)S(1)}, u32[]{:S(2)}, u32[]{:S(2)}) collective-permute-start(f32[128,256]{1,0:T(8,128)S(1)} %get-tuple-element.20), channel_id=1, source_target_pairs={{0,2},{2,4},{4,6},{6,8},{8,10},{10,12},{12,14},{14,0},{1,3},{3,5},... | collective-permute-start | bytes 393224 | tf_op jit(solution)/shard_map/reduce_a/ppermute | solution.py:18
  96.1 4.4 %collective-permute-start.17 = (f32[64,256]{1,0:T(8,128)S(1)}, f32[64,256]{1,0:T(8,128)S(1)}, u32[]{:S(2)}, u32[]{:S(2)}) collective-permute-start(f32[64,256]{1,0:T(8,128)S(1)} %get-tuple-element.48), channel_id=1, source_target_pairs={{0,16},{16,32},{32,48},{48,0},{1,17},{17,33},{33,49},{49,1},{2,18}... | collective-permute-start | bytes 196616 | tf_op jit(solution)/shard_map/reduce_b2/ppermute | solution.py:18
  96.2 4.3 %collective-permute-start.19 = (f32[64,256]{1,0:T(8,128)S(1)}, f32[64,256]{1,0:T(8,128)S(1)}, u32[]{:S(2)}, u32[]{:S(2)}) collective-permute-start(f32[64,256]{1,0:T(8,128)S(1)} %get-tuple-element.50), channel_id=1, source_target_pairs={{0,48},{16,0},{32,16},{48,32},{1,49},{17,1},{33,17},{49,33},{2,50}... | collective-permute-start | bytes 196616 | tf_op jit(solution)/shard_map/reduce_b2/ppermute | solution.py:18
  98.9 5.7 %collective-permute-start.13 = (f32[128,256]{1,0:T(8,128)S(1)}, f32[128,256]{1,0:T(8,128)S(1)}, u32[]{:S(2)}, u32[]{:S(2)}) collective-permute-start(f32[128,256]{1,0:T(8,128)S(1)} %bitcast_add_fusion.2), channel_id=1, source_target_pairs={{0,14},{2,0},{4,2},{6,4},{8,6},{10,8},{12,10},{14,12},{1,15},{3,1}... | collective-permute-start | bytes 393224 | tf_op jit(solution)/shard_map/reduce_a/ppermute | solution.py:18
  101.4 7.7 %collective-permute-start.20 = (f32[128,256]{1,0:T(8,128)S(1)}, f32[128,256]{1,0:T(8,128)S(1)}, u32[]{:S(2)}, u32[]{:S(2)}) collective-permute-start(f32[128,256]{1,0:T(8,128)S(1)} %pad_maximum_fusion.11), channel_id=1, source_target_pairs={{0,48},{16,0},{32,16},{48,32},{1,49},{17,1},{33,17},{49,33},{2,50}... | collective-permute-start | bytes 393224 | tf_op jit(solution)/shard_map/reduce_b2/ppermute | solution.py:18
  104.5 5.1 %collective-permute-start.18 = (f32[128,256]{1,0:T(8,128)S(1)}, f32[128,256]{1,0:T(8,128)S(1)}, u32[]{:S(2)}, u32[]{:S(2)}) collective-permute-start(f32[128,256]{1,0:T(8,128)S(1)} %pad_maximum_fusion.10), channel_id=1, source_target_pairs={{0,16},{16,32},{32,48},{48,0},{1,17},{17,33},{33,49},{49,1},{2,18}... | collective-permute-start | bytes 393224 | tf_op jit(solution)/shard_map/reduce_b2/ppermute | solution.py:18
  104.7 60.2 %copy-start.3 = (f32[128,512]{1,0:T(8,128)S(1)}, f32[128,512]{1,0:T(8,128)}, u32[]{:S(2)}) copy-start(f32[128,512]{1,0:T(8,128)} %param.7) | copy-start | bytes 786436
  104.7 60.2 %copy-start.4 = (f32[128,512]{1,0:T(8,128)S(1)}, f32[128,512]{1,0:T(8,128)}, u32[]{:S(2)}) copy-start(f32[128,512]{1,0:T(8,128)} %param.8) | copy-start | bytes 786436
  104.7 60.2 %copy-start.5 = (f32[128,512]{1,0:T(8,128)S(1)}, f32[128,512]{1,0:T(8,128)}, u32[]{:S(2)}) copy-start(f32[128,512]{1,0:T(8,128)} %param.9) | copy-start | bytes 786436
  104.7 9.6 %collective-permute-start.16 = (f32[128,256]{1,0:T(8,128)S(1)}, f32[128,256]{1,0:T(8,128)S(1)}, u32[]{:S(2)}, u32[]{:S(2)}) collective-permute-start(f32[128,256]{1,0:T(8,128)S(1)} %fusion.20), channel_id=1, source_target_pairs={{0,128},{64,192},{128,0},{192,64},{1,129},{65,193},{129,1},{193,65... | collective-permute-start | bytes 393224 | tf_op jit(solution)/shard_map/members/ppermute | solution.py:18
  107.7 7.3 %collective-permute-start.15 = (f32[128,256]{1,0:T(8,128)S(1)}, f32[128,256]{1,0:T(8,128)S(1)}, u32[]{:S(2)}, u32[]{:S(2)}) collective-permute-start(f32[128,256]{1,0:T(8,128)S(1)} %fusion.20), channel_id=1, source_target_pairs={{0,192},{64,0},{128,64},{192,128},{1,193},{65,1},{129,65},{193,129... | collective-permute-start | bytes 393224 | tf_op jit(solution)/shard_map/members/ppermute | solution.py:18
  108.5 6.5 %collective-permute-start.14 = (f32[128,256]{1,0:T(8,128)S(1)}, f32[128,256]{1,0:T(8,128)S(1)}, u32[]{:S(2)}, u32[]{:S(2)}) collective-permute-start(f32[128,256]{1,0:T(8,128)S(1)} %fusion.20), channel_id=1, source_target_pairs={{0,64},{64,128},{128,192},{192,0},{1,65},{65,129},{129,193},{193,1... | collective-permute-start | bytes 393224 | tf_op jit(solution)/shard_map/members/ppermute | solution.py:18
  110.5 6.2 %collective-permute-start.23 = (f32[128,256]{1,0:T(8,128)S(1)}, f32[128,256]{1,0:T(8,128)S(1)}, u32[]{:S(2)}, u32[]{:S(2)}) collective-permute-start(f32[128,256]{1,0:T(8,128)S(1)} %fusion.19), channel_id=1, source_target_pairs={{0,128},{64,192},{128,0},{192,64},{1,129},{65,193},{129,1},{193,65... | collective-permute-start | bytes 393224 | tf_op jit(solution)/shard_map/members/ppermute | solution.py:18
  113.5 5.6 %collective-permute-start.22 = (f32[128,256]{1,0:T(8,128)S(1)}, f32[128,256]{1,0:T(8,128)S(1)}, u32[]{:S(2)}, u32[]{:S(2)}) collective-permute-start(f32[128,256]{1,0:T(8,128)S(1)} %fusion.19), channel_id=1, source_target_pairs={{0,192},{64,0},{128,64},{192,128},{1,193},{65,1},{129,65},{193,129... | collective-permute-start | bytes 393224 | tf_op jit(solution)/shard_map/members/ppermute | solution.py:18
  114.3 5.1 %collective-permute-start.21 = (f32[128,256]{1,0:T(8,128)S(1)}, f32[128,256]{1,0:T(8,128)S(1)}, u32[]{:S(2)}, u32[]{:S(2)}) collective-permute-start(f32[128,256]{1,0:T(8,128)S(1)} %fusion.19), channel_id=1, source_target_pairs={{0,64},{64,128},{128,192},{192,0},{1,65},{65,129},{129,193},{193,1... | collective-permute-start | bytes 393224 | tf_op jit(solution)/shard_map/members/ppermute | solution.py:18
  (1 other events, 1.4 us)
Sparse Core Ops, SparseCore 0:
  27.5 56.9 reduce-scatter.1
  166.2 75.7 all-gather.1
where the time goes:
time: 257 us; the launch traced here: 256 us
  waiting for transfers between devices  130 us (51%)
  starting transfers between devices  33.6 us (13%)
  between operations  26 us (10%)
  blocking collectives  25.9 us (10%)
  local copies, waits for them, and re-layouts  25.2 us (10%)
  other arithmetic  7.97 us (3%)
  matrix products  6.9 us (3%)
    all_gather x1, waiting for transfers between devices, local(): lax.all_gather(new_master.astype(jnp.bfloat16), GROUP, axis=0, tiled=True)  75.9 us
    ppermute x24, waiting for transfers between devices, shifted(): lax.ppermute(value, axis, [(i, (i + step) % size) for i in range(size)])  54.5 us
    ppermute x24, starting transfers between devices, shifted(): lax.ppermute(value, axis, [(i, (i + step) % size) for i in range(size)])  33.6 us
    all_to_all x1, blocking collectives, local(): everyone = lax.all_to_all(jnp.broadcast_to(row, (64, 1, 128)), GROUP, 0, 0)  25.9 us
    unnamed x17, local copies, waits for them, and re-layouts  13.8 us
    dot_general x5, matrix products, product(): lax.dot_general(grad_columns, act_columns, contract_first, preferred_elem...  6.9 us
    concatenate x1, local copies, waits for them, and re-layouts, local(): jnp.concatenate([jnp.stack(sums), jnp.zeros((128 - len(sums),), jnp.float...  6.4 us
  transfers between devices with their start and end apart: 26, of which 13 were waited for; matrix products, arithmetic and copies ran while one was open for 4% of the time, Pallas kernels for 0%

commit v1 on v0

--- a/solution.py
+++ b/solution.py
@@ -150,7 +150,11 @@
         )
         new_master = master - learn_rate * update
     with jax.named_scope("params"):
-        params = lax.all_gather(new_master.astype(jnp.bfloat16), GROUP, axis=0, tiled=True)
+        part_2 = new_master.astype(jnp.bfloat16)
+        peers = lax.axis_size(GROUP)
+        blocks = jnp.stack([part_2 for _ in range(peers)])
+        blocks = lax.all_to_all(blocks, GROUP, split_axis=0, concat_axis=0)
+        params = jnp.concatenate(blocks, axis=0)
     return (new_master, new_first, new_second, params)
 
 

time: 257 us -> 372 us (1.45)
  blocking collectives: 25.9 us -> 217 us
  waiting for transfers between devices: 130 us -> 54.5 us
    all_to_all x0 -> x1, blocking collectives: none -> 191 us  [local(): blocks = lax.all_to_all(blocks, GROUP, split_axis=0, concat_axis=0)]
    all_gather x1 -> x0, waiting for transfers between devices: 75.9 us -> none  [local(): lax.all_gather(new_master.astype(jnp.bfloat16), GROUP, axis=0, tiled=True)]
  transfers between devices with their start and end apart: 26 -> 25, of which waited for: 13 -> 11; matrix products, arithmetic and copies ran while one was open for 4% -> 3% of each run, Pallas kernels for 0% -> 0%
where the time goes in v1:
time: 372 us
  blocking collectives  217 us (58%)
  waiting for transfers between devices  54.5 us (15%)
  starting transfers between devices  33.6 us (9%)
  local copies, waits for them, and re-layouts  26.1 us (7%)
  between operations  25.7 us (7%)
  other arithmetic  7.89 us (2%)
  matrix products  6.9 us (2%)
    all_to_all x1, blocking collectives, local(): blocks = lax.all_to_all(blocks, GROUP, split_axis=0, concat_axis=0)  191 us
    ppermute x24, waiting for transfers between devices, shifted(): lax.ppermute(value, axis, [(i, (i + step) % size) for i in range(size)])  54.5 us
    ppermute x24, starting transfers between devices, shifted(): lax.ppermute(value, axis, [(i, (i + step) % size) for i in range(size)])  33.6 us
    all_to_all x1, blocking collectives, local(): everyone = lax.all_to_all(jnp.broadcast_to(row, (64, 1, 128)), GROUP, 0, 0)  25.9 us
    unnamed x17, local copies, waits for them, and re-layouts  13.8 us
  transfers between devices with their start and end apart: 25, of which 11 were waited for; matrix products, arithmetic and copies ran while one was open for 3% of the time, Pallas kernels for 0%

profile of v1, /device:TPU:1, one launch (start us, length us, event | category | flops | bytes accessed | tf_op | source)
XLA Modules:
  0.0 371.6 jit_solution(11007948250555621606)
XLA Ops:
  7.2 6.4 %copy.14 = bf16[256,8192]{0,1:T(8,128)(2,1)} copy(bf16[256,8192]{1,0:T(8,128)(2,1)} %param.6) | data formatting | bytes 8388608 | tf_op args[1]
  13.6 2.5 broadcast_select_fusion.1
  16.1 3.3 collective-permute-start
  19.6 4.0 %collective-permute-done.1 = bf16[256,512]{1,0:T(8,128)(2,1)S(1)} collective-permute-done((bf16[256,512]{1,0:T(8,128)(2,1)S(1)}, bf16[256,512]{1,0:T(8,128)(2,1)S(1)}, u32[]{:S(2)}, u32[]{:S(2)}) %collective-permute-start.1) | collective-permute-done | bytes 262176 | tf_op jit(solution)/shard_map/core_swap/ppermute | solution.py:18
  23.7 1.3 fusion
  25.0 2.3 copy.15
  27.4 1.5 fusion.8
  31.4 1.5 fusion.5
  33.3 10.0 %collective-permute-done.4 = f32[512,256]{1,0:T(8,128)S(1)} collective-permute-done((f32[512,256]{1,0:T(8,128)}, f32[512,256]{1,0:T(8,128)S(1)}, u32[]{:S(2)}, u32[]{:S(2)}) %collective-permute-start.4) | collective-permute-done | bytes 524320 | tf_op jit(solution)/shard_map/reduce_a/ppermute | solution.py:18
  43.5 1.9 collective-permute-start.5
  46.6 20.7 %collective-permute-done.5 = f32[1024,256]{1,0:T(8,128)} collective-permute-done((f32[1024,256]{1,0:T(8,128)S(1)}, f32[1024,256]{1,0:T(8,128)}, u32[]{:S(2)}, u32[]{:S(2)}) %collective-permute-start.5) | collective-permute-done | bytes 1048608 | tf_op jit(solution)/shard_map/reduce_a/ppermute | solution.py:18
  67.3 4.0 %collective-permute-done.3 = f32[1024,256]{1,0:T(8,128)} collective-permute-done((f32[1024,256]{1,0:T(8,128)}, f32[1024,256]{1,0:T(8,128)}, u32[]{:S(2)}, u32[]{:S(2)}) %collective-permute-start.3) | collective-permute-done | bytes 1048608 | tf_op jit(solution)/shard_map/reduce_a/ppermute | solution.py:18
  71.3 2.2 fusion.1
  73.6 1.7 collective-permute-start.6
  75.3 4.3 %collective-permute-start.10 = (f32[64,256]{1,0:T(8,128)S(1)}, f32[64,256]{1,0:T(8,128)S(1)}, u32[]{:S(2)}, u32[]{:S(2)}) collective-permute-start(f32[64,256]{1,0:T(8,128)S(1)} %get-tuple-element.26), channel_id=1, source_target_pairs={{0,14},{2,0},{4,2},{6,4},{8,6},{10,8},{12,10},{14,12},{1,15},{3,1}... | collective-permute-start | bytes 196616 | tf_op jit(solution)/shard_map/reduce_a/ppermute | solution.py:18
  79.6 3.5 collective-permute-done.6
  83.3 2.7 collective-permute-start.11
  86.0 2.3 collective-permute-done.7
  88.6 5.0 %collective-permute-done.8 = f32[128,256]{1,0:T(8,128)S(1)} collective-permute-done((f32[128,256]{1,0:T(8,128)S(1)}, f32[128,256]{1,0:T(8,128)S(1)}, u32[]{:S(2)}, u32[]{:S(2)}) %collective-permute-start.8) | collective-permute-done | bytes 131104 | tf_op jit(solution)/shard_map/reduce_a/ppermute | solution.py:18
  93.8 1.4 collective-permute-start.9
  96.2 2.7 collective-permute-start.19
  98.9 1.5 collective-permute-start.13
  101.4 3.0 collective-permute-start.20
  104.7 3.0 collective-permute-start.16
  110.5 3.0 collective-permute-start.23
  115.0 1.7 collective-permute-done.23
  116.8 2.6 collective-permute-done.22
  120.3 6.3 %concatenate.51 = f32[128]{0:T(128)S(1)} concatenate(f32[1]{0:T(128)} %bitcast.26, f32[1]{0:T(128)} %bitcast.27, f32[1]{0:T(128)} %bitcast.28, f32[1]{0:T(128)} %bitcast.29, f32[1]{0:T(128)} %bitcast.30, f32[1]{0:T(128)} %bitcast.31, f32[1]{0:T(128)} %bitcast.32, f32[1]{0:T(128)} %bitcast.33, f32[1]{0:T(128)} %bitcast.34, f32[1]{0:T(128)} %bitcast.35, f32[118]{0:T(128)S(1)} %broadcast_in_dim.6), dimensions={0} | concatenate | bytes 1024 | tf_op jit(solution)/shard_map/gram/concatenate | solution.py:128
  126.6 25.9 %all_to_all.10 = f32[64,1,128]{2,1,0:T(1,128)S(1)} all-to-all(f32[64,1,128]{2,1,0:T(1,128)S(1)} %broadcast_in_dim.7), channel_id=1, replica_groups=mesh['rep'=4,'x'=4,'z'=8,'core'=2] {'x','z','core'}, dimensions={0} | all-to-all | bytes 65536 | tf_op jit(solution)/shard_map/gram/all_to_all | solution.py:129
  164.5 1.1 fusion.34
  166.6 190.8 %all_to_all.11 = bf16[64,128,512]{2,1,0:T(8,128)(2,1)} all-to-all(bf16[64,128,512]{2,1,0:T(8,128)(2,1)S(1)} %stack.32), channel_id=1, replica_groups=mesh['rep'=4,'x'=4,'z'=8,'core'=2] {'x','z','core'}, dimensions={0} | all-to-all | bytes 16777216 | tf_op jit(solution)/shard_map/params/all_to_all | solution.py:156
  357.4 7.3 %copy.19 = bf16[8192,512]{1,0:T(8,128)(2,1)} copy(bf16[8192,512]{1,0:T(8,128)(2,1)} %bitcast.84) | data formatting | bytes 16777216
  (74 shorter events, 14.4 us)
Async XLA Ops:
  7.2 88.0 %reduce-scatter.2.cloned.1.call-start = ((), (), s32[]{:S(2)}) async-start(), calls=%async_computation.3 | async-start | bytes 4718592 | tf_op jit(solution)/shard_map/reduce_b/reduce_scatter | solution.py:109
  13.6 5.9 %copy-start.6 = (bf16[256,512]{1,0:T(8,128)(2,1)S(1)}, bf16[256,512]{1,0:T(8,128)(2,1)}, u32[]{:S(2)}) copy-start(bf16[256,512]{1,0:T(8,128)(2,1)} %param.5) | copy-start | bytes 786436
  16.1 7.5 %collective-permute-start = (bf16[256,4096]{0,1:T(8,128)(2,1)S(1)}, bf16[256,4096]{0,1:T(8,128)(2,1)S(1)}, u32[]{:S(2)}, u32[]{:S(2)}) collective-permute-start(bf16[256,4096]{0,1:T(8,128)(2,1)S(1)} %bitcast.94), channel_id=1, source_target_pairs={{0,1},{1,0},{2,3},{3,2},{4,5},{5,4},{6,7},{7,6},{8,9},{9,8},{10,11... | collective-permute-start | bytes 6291464 | tf_op jit(solution)/shard_map/core_swap/ppermute | solution.py:18
  19.5 4.2 %collective-permute-start.1 = (bf16[256,512]{1,0:T(8,128)(2,1)S(1)}, bf16[256,512]{1,0:T(8,128)(2,1)S(1)}, u32[]{:S(2)}, u32[]{:S(2)}) collective-permute-start(bf16[256,512]{1,0:T(8,128)(2,1)S(1)} %copy-done.6), channel_id=1, source_target_pairs={{0,1},{1,0},{2,3},{3,2},{4,5},{5,4},{6,7},{7,6},{8,9},{9,8},{10,11... | collective-permute-start | bytes 786440 | tf_op jit(solution)/shard_map/core_swap/ppermute | solution.py:18
  23.6 9.2 %copy-start.2 = (bf16[512,512]{1,0:T(8,128)(2,1)}, bf16[512,512]{1,0:T(8,128)(2,1)S(1)}, u32[]{:S(2)}) copy-start(bf16[512,512]{1,0:T(8,128)(2,1)S(1)} %constant_dynamic-update-slice_fusion) | copy-start | bytes 1572868
  23.7 1.4 copy-start
  29.9 13.4 %collective-permute-start.4 = (f32[512,256]{1,0:T(8,128)}, f32[512,256]{1,0:T(8,128)S(1)}, u32[]{:S(2)}, u32[]{:S(2)}) collective-permute-start(f32[512,256]{1,0:T(8,128)} %get-tuple-element.31), channel_id=1, source_target_pairs={{0,48},{16,0},{32,16},{48,32},{1,49},{17,1},{33,17},{49,33},{2,50}... | collective-permute-start | bytes 1572872 | tf_op jit(solution)/shard_map/reduce_a/ppermute | solution.py:18
  30.6 2.2 copy-start.1
  30.6 14.8 %collective-permute-start.2 = (f32[512,256]{1,0:T(8,128)}, f32[512,256]{1,0:T(8,128)S(1)}, u32[]{:S(2)}, u32[]{:S(2)}) collective-permute-start(f32[512,256]{1,0:T(8,128)} %get-tuple-element.30), channel_id=1, source_target_pairs={{0,16},{16,32},{32,48},{48,0},{1,17},{17,33},{33,49},{49,1},{2,18}... | collective-permute-start | bytes 1572872 | tf_op jit(solution)/shard_map/reduce_a/ppermute | solution.py:18
  43.5 23.7 %collective-permute-start.5 = (f32[1024,256]{1,0:T(8,128)S(1)}, f32[1024,256]{1,0:T(8,128)}, u32[]{:S(2)}, u32[]{:S(2)}) collective-permute-start(f32[1024,256]{1,0:T(8,128)S(1)} %pad_maximum_fusion.3), channel_id=1, source_target_pairs={{0,48},{16,0},{32,16},{48,32},{1,49},{17,1},{33,17},{49,33},{2,50}... | collective-permute-start | bytes 3145736 | tf_op jit(solution)/shard_map/reduce_a/ppermute | solution.py:18
  46.6 24.7 %collective-permute-start.3 = (f32[1024,256]{1,0:T(8,128)}, f32[1024,256]{1,0:T(8,128)}, u32[]{:S(2)}, u32[]{:S(2)}) collective-permute-start(f32[1024,256]{1,0:T(8,128)} %pad_maximum_fusion.2), channel_id=1, source_target_pairs={{0,16},{16,32},{32,48},{48,0},{1,17},{17,33},{33,49},{49,1},{2,18}... | collective-permute-start | bytes 3145736 | tf_op jit(solution)/shard_map/reduce_a/ppermute | solution.py:18
  73.6 9.5 %collective-permute-start.6 = (f32[64,256]{1,0:T(8,128)S(1)}, f32[64,256]{1,0:T(8,128)S(1)}, u32[]{:S(2)}, u32[]{:S(2)}) collective-permute-start(f32[64,256]{1,0:T(8,128)S(1)} %get-tuple-element.24), channel_id=1, source_target_pairs={{0,2},{2,4},{4,6},{6,8},{8,10},{10,12},{12,14},{14,0},{1,3},{3,5},... | collective-permute-start | bytes 196616 | tf_op jit(solution)/shard_map/reduce_a/ppermute | solution.py:18
  75.3 7.8 %collective-permute-start.10 = (f32[64,256]{1,0:T(8,128)S(1)}, f32[64,256]{1,0:T(8,128)S(1)}, u32[]{:S(2)}, u32[]{:S(2)}) collective-permute-start(f32[64,256]{1,0:T(8,128)S(1)} %get-tuple-element.26), channel_id=1, source_target_pairs={{0,14},{2,0},{4,2},{6,4},{8,6},{10,8},{12,10},{14,12},{1,15},{3,1}... | collective-permute-start | bytes 196616 | tf_op jit(solution)/shard_map/reduce_a/ppermute | solution.py:18
  83.1 5.1 %collective-permute-start.7 = (f32[128,256]{1,0:T(8,128)S(1)}, f32[128,256]{1,0:T(8,128)S(1)}, u32[]{:S(2)}, u32[]{:S(2)}) collective-permute-start(f32[128,256]{1,0:T(8,128)S(1)} %pad_maximum_fusion.8), channel_id=1, source_target_pairs={{0,2},{2,4},{4,6},{6,8},{8,10},{10,12},{12,14},{14,0},{1,3},{3,5},... | collective-permute-start | bytes 393224 | tf_op jit(solution)/shard_map/reduce_a/ppermute | solution.py:18
  83.3 5.3 %collective-permute-start.11 = (f32[128,256]{1,0:T(8,128)S(1)}, f32[128,256]{1,0:T(8,128)S(1)}, u32[]{:S(2)}, u32[]{:S(2)}) collective-permute-start(f32[128,256]{1,0:T(8,128)S(1)} %pad_maximum_fusion.9), channel_id=1, source_target_pairs={{0,14},{2,0},{4,2},{6,4},{8,6},{10,8},{12,10},{14,12},{1,15},{3,1}... | collective-permute-start | bytes 393224 | tf_op jit(solution)/shard_map/reduce_a/ppermute | solution.py:18
  88.3 5.3 %collective-permute-start.8 = (f32[128,256]{1,0:T(8,128)S(1)}, f32[128,256]{1,0:T(8,128)S(1)}, u32[]{:S(2)}, u32[]{:S(2)}) collective-permute-start(f32[128,256]{1,0:T(8,128)S(1)} %bitcast_add_fusion.3), channel_id=1, source_target_pairs={{0,2},{2,4},{4,6},{6,8},{8,10},{10,12},{12,14},{14,0},{1,3},{3,5},... | collective-permute-start | bytes 393224 | tf_op jit(solution)/shard_map/reduce_a/ppermute | solution.py:18
  93.6 5.3 %collective-permute-start.12 = (f32[128,256]{1,0:T(8,128)S(1)}, f32[128,256]{1,0:T(8,128)S(1)}, u32[]{:S(2)}, u32[]{:S(2)}) collective-permute-start(f32[128,256]{1,0:T(8,128)S(1)} %get-tuple-element.21), channel_id=1, source_target_pairs={{0,14},{2,0},{4,2},{6,4},{8,6},{10,8},{12,10},{14,12},{1,15},{3,1}... | collective-permute-start | bytes 393224 | tf_op jit(solution)/shard_map/reduce_a/ppermute | solution.py:18
  93.8 10.8 %collective-permute-start.9 = (f32[128,256]{1,0:T(8,128)S(1)}, f32[128,256]{1,0:T(8,128)S(1)}, u32[]{:S(2)}, u32[]{:S(2)}) collective-permute-start(f32[128,256]{1,0:T(8,128)S(1)} %get-tuple-element.20), channel_id=1, source_target_pairs={{0,2},{2,4},{4,6},{6,8},{8,10},{10,12},{12,14},{14,0},{1,3},{3,5},... | collective-permute-start | bytes 393224 | tf_op jit(solution)/shard_map/reduce_a/ppermute | solution.py:18
  96.1 4.4 %collective-permute-start.17 = (f32[64,256]{1,0:T(8,128)S(1)}, f32[64,256]{1,0:T(8,128)S(1)}, u32[]{:S(2)}, u32[]{:S(2)}) collective-permute-start(f32[64,256]{1,0:T(8,128)S(1)} %get-tuple-element.48), channel_id=1, source_target_pairs={{0,16},{16,32},{32,48},{48,0},{1,17},{17,33},{33,49},{49,1},{2,18}... | collective-permute-start | bytes 196616 | tf_op jit(solution)/shard_map/reduce_b2/ppermute | solution.py:18
  96.2 4.3 %collective-permute-start.19 = (f32[64,256]{1,0:T(8,128)S(1)}, f32[64,256]{1,0:T(8,128)S(1)}, u32[]{:S(2)}, u32[]{:S(2)}) collective-permute-start(f32[64,256]{1,0:T(8,128)S(1)} %get-tuple-element.50), channel_id=1, source_target_pairs={{0,48},{16,0},{32,16},{48,32},{1,49},{17,1},{33,17},{49,33},{2,50}... | collective-permute-start | bytes 196616 | tf_op jit(solution)/shard_map/reduce_b2/ppermute | solution.py:18
  98.9 5.7 %collective-permute-start.13 = (f32[128,256]{1,0:T(8,128)S(1)}, f32[128,256]{1,0:T(8,128)S(1)}, u32[]{:S(2)}, u32[]{:S(2)}) collective-permute-start(f32[128,256]{1,0:T(8,128)S(1)} %bitcast_add_fusion.2), channel_id=1, source_target_pairs={{0,14},{2,0},{4,2},{6,4},{8,6},{10,8},{12,10},{14,12},{1,15},{3,1}... | collective-permute-start | bytes 393224 | tf_op jit(solution)/shard_map/reduce_a/ppermute | solution.py:18
  101.4 7.7 %collective-permute-start.20 = (f32[128,256]{1,0:T(8,128)S(1)}, f32[128,256]{1,0:T(8,128)S(1)}, u32[]{:S(2)}, u32[]{:S(2)}) collective-permute-start(f32[128,256]{1,0:T(8,128)S(1)} %pad_maximum_fusion.11), channel_id=1, source_target_pairs={{0,48},{16,0},{32,16},{48,32},{1,49},{17,1},{33,17},{49,33},{2,50}... | collective-permute-start | bytes 393224 | tf_op jit(solution)/shard_map/reduce_b2/ppermute | solution.py:18
  104.5 5.1 %collective-permute-start.18 = (f32[128,256]{1,0:T(8,128)S(1)}, f32[128,256]{1,0:T(8,128)S(1)}, u32[]{:S(2)}, u32[]{:S(2)}) collective-permute-start(f32[128,256]{1,0:T(8,128)S(1)} %pad_maximum_fusion.10), channel_id=1, source_target_pairs={{0,16},{16,32},{32,48},{48,0},{1,17},{17,33},{33,49},{49,1},{2,18}... | collective-permute-start | bytes 393224 | tf_op jit(solution)/shard_map/reduce_b2/ppermute | solution.py:18
  104.6 59.8 %copy-start.3 = (f32[128,512]{1,0:T(8,128)S(1)}, f32[128,512]{1,0:T(8,128)}, u32[]{:S(2)}) copy-start(f32[128,512]{1,0:T(8,128)} %param.7) | copy-start | bytes 786436
  104.6 59.8 %copy-start.4 = (f32[128,512]{1,0:T(8,128)S(1)}, f32[128,512]{1,0:T(8,128)}, u32[]{:S(2)}) copy-start(f32[128,512]{1,0:T(8,128)} %param.8) | copy-start | bytes 786436
  104.6 59.8 %copy-start.5 = (f32[128,512]{1,0:T(8,128)S(1)}, f32[128,512]{1,0:T(8,128)}, u32[]{:S(2)}) copy-start(f32[128,512]{1,0:T(8,128)} %param.9) | copy-start | bytes 786436
  104.7 9.6 %collective-permute-start.16 = (f32[128,256]{1,0:T(8,128)S(1)}, f32[128,256]{1,0:T(8,128)S(1)}, u32[]{:S(2)}, u32[]{:S(2)}) collective-permute-start(f32[128,256]{1,0:T(8,128)S(1)} %fusion.20), channel_id=1, source_target_pairs={{0,128},{64,192},{128,0},{192,64},{1,129},{65,193},{129,1},{193,65... | collective-permute-start | bytes 393224 | tf_op jit(solution)/shard_map/members/ppermute | solution.py:18
  107.7 7.3 %collective-permute-start.15 = (f32[128,256]{1,0:T(8,128)S(1)}, f32[128,256]{1,0:T(8,128)S(1)}, u32[]{:S(2)}, u32[]{:S(2)}) collective-permute-start(f32[128,256]{1,0:T(8,128)S(1)} %fusion.20), channel_id=1, source_target_pairs={{0,192},{64,0},{128,64},{192,128},{1,193},{65,1},{129,65},{193,129... | collective-permute-start | bytes 393224 | tf_op jit(solution)/shard_map/members/ppermute | solution.py:18
  108.4 6.5 %collective-permute-start.14 = (f32[128,256]{1,0:T(8,128)S(1)}, f32[128,256]{1,0:T(8,128)S(1)}, u32[]{:S(2)}, u32[]{:S(2)}) collective-permute-start(f32[128,256]{1,0:T(8,128)S(1)} %fusion.20), channel_id=1, source_target_pairs={{0,64},{64,128},{128,192},{192,0},{1,65},{65,129},{129,193},{193,1... | collective-permute-start | bytes 393224 | tf_op jit(solution)/shard_map/members/ppermute | solution.py:18
  110.5 6.2 %collective-permute-start.23 = (f32[128,256]{1,0:T(8,128)S(1)}, f32[128,256]{1,0:T(8,128)S(1)}, u32[]{:S(2)}, u32[]{:S(2)}) collective-permute-start(f32[128,256]{1,0:T(8,128)S(1)} %fusion.19), channel_id=1, source_target_pairs={{0,128},{64,192},{128,0},{192,64},{1,129},{65,193},{129,1},{193,65... | collective-permute-start | bytes 393224 | tf_op jit(solution)/shard_map/members/ppermute | solution.py:18
  113.5 5.8 %collective-permute-start.22 = (f32[128,256]{1,0:T(8,128)S(1)}, f32[128,256]{1,0:T(8,128)S(1)}, u32[]{:S(2)}, u32[]{:S(2)}) collective-permute-start(f32[128,256]{1,0:T(8,128)S(1)} %fusion.19), channel_id=1, source_target_pairs={{0,192},{64,0},{128,64},{192,128},{1,193},{65,1},{129,65},{193,129... | collective-permute-start | bytes 393224 | tf_op jit(solution)/shard_map/members/ppermute | solution.py:18
  114.3 5.1 %collective-permute-start.21 = (f32[128,256]{1,0:T(8,128)S(1)}, f32[128,256]{1,0:T(8,128)S(1)}, u32[]{:S(2)}, u32[]{:S(2)}) collective-permute-start(f32[128,256]{1,0:T(8,128)S(1)} %fusion.19), channel_id=1, source_target_pairs={{0,64},{64,128},{128,192},{192,0},{1,65},{65,129},{129,193},{193,1... | collective-permute-start | bytes 393224 | tf_op jit(solution)/shard_map/members/ppermute | solution.py:18
Sparse Core Ops, SparseCore 0:
  27.5 57.0 reduce-scatter.1
